TPU v7x, 32 devices: a whole 2x2x4 slice. The times are simulated.
32 devices in a mesh: layer: 4 (over y, x), col: 8 (over z, core).
Axes of the slice: x: 2, y: 2, z: 4, core: 2. Of those that a mesh axis runs over, the one named last changes fastest.
Arguments:
- inputs: bfloat16 [4, 128, 4096], replicated, may hold values from -6 to 6
- w_input: bfloat16 [4, 4096, 4, 4096], P('layer', None, None, 'col'), may hold values from -0.09375 to 0.09375
- w_recur: bfloat16 [4, 4096, 4, 4096], P('layer', None, None, 'col'), may hold values from -0.09375 to 0.09375
- bias: float32 [4, 4, 4096], P('layer', None, 'col'), may hold values from -1 to 2
- h_start: bfloat16 [4, 128, 4096], P('layer', None, 'col'), may hold values from -3 to 3
- c_start: float32 [4, 128, 4096], P('layer', None, 'col'), may hold values from -6 to 6
Outputs:
- hidden_seq: bfloat16 [4, 4, 128, 4096], P('layer', None, None, 'col')
- cell_final: float32 [4, 128, 4096], P('layer', None, 'col')
All inputs are finite; a program needn't handle non-finite values.
Results may differ from a plain program's by a relative error of at most 0.0024.
Values may be sent and summed in bfloat16 or wider, within the bound.
A program may use at most 128 MiB of HBM per device.

v0:
```python
import jax
import jax.numpy as jnp
from jax import lax
from jax.sharding import PartitionSpec as P


def passed_along(value, axis, steps):
    count = lax.axis_size(axis)
    first, last = (max(0, -steps), min(count, count - steps))
    return lax.ppermute(value, axis, [(source, source + steps) for source in range(first, last)])


def body(inputs, w_input, w_recur, bias, h_start, c_start):
    steps = inputs.shape[0]
    batch = inputs.shape[1]
    width = inputs.shape[2]
    local = w_input.shape[3]
    span = steps // 4
    count = steps // span
    groups = lax.axis_size("layer")
    rounds = count + groups - 1
    section = lax.axis_index("layer")
    weight_in = w_input[0].reshape(width, 4 * local)
    weight_rec = w_recur[0].reshape(width, 4 * local)
    offset = bias[0].reshape(4 * local)
    hidden_full = lax.all_gather(h_start[0], "col", axis=1, tiled=True)
    cell = c_start[0]
    sequence = jnp.zeros((steps, batch, local), jnp.bfloat16)
    arrived = jnp.zeros((span, batch, width), jnp.bfloat16)

    def advance(carry, z_in):
        hidden_prev, cell_prev = carry
        gates = z_in + jnp.dot(hidden_prev, weight_rec, preferred_element_type=jnp.float32)
        gates = gates.reshape(batch, 4, local)
        cell_new = jax.nn.sigmoid(gates[:, 1]) * cell_prev + jax.nn.sigmoid(gates[:, 0]) * jnp.tanh(
            gates[:, 2]
        )
        hidden_new = (jax.nn.sigmoid(gates[:, 3]) * jnp.tanh(cell_new)).astype(jnp.bfloat16)
        hidden_wide = lax.all_gather(hidden_new, "col", axis=1, tiled=True)
        return ((hidden_wide, cell_new), (hidden_new, hidden_wide))

    for turn in range(rounds):
        block_id = turn - section
        valid = jnp.logical_and(block_id >= 0, block_id < count)
        start = jnp.clip(block_id, 0, count - 1) * span
        own_block = lax.dynamic_slice_in_dim(inputs, start, span, 0)
        source = jnp.where(section == 0, own_block, arrived)
        projected = (
            jnp.dot(
                source.reshape(span * batch, width), weight_in, preferred_element_type=jnp.float32
            )
            + offset
        )
        projected = projected.reshape(span, batch, 4 * local)
        (hidden_next, cell_next), (shards, wides) = lax.scan(
            advance, (hidden_full, cell), projected
        )
        hidden_full = jnp.where(valid, hidden_next, hidden_full)
        cell = jnp.where(valid, cell_next, cell)
        sequence = jnp.where(
            valid, lax.dynamic_update_slice_in_dim(sequence, shards, start, 0), sequence
        )
        if turn + 1 < rounds:
            received = passed_along(shards, "layer", 1)
            arrived = lax.all_gather(received, "col", axis=2, tiled=True)
    return (sequence[None], cell[None])


def solution(mesh):
    in_specs = (
        P(),
        P("layer", None, None, "col"),
        P("layer", None, None, "col"),
        P("layer", None, "col"),
        P("layer", None, "col"),
        P("layer", None, "col"),
    )
    out_specs = (P("layer", None, None, "col"), P("layer", None, "col"))
    return jax.shard_map(body, mesh=mesh, in_specs=in_specs, out_specs=out_specs, check_vma=False)
```

profile of v0, /device:TPU:0, one launch (start us, length us, event | category | flops | bytes accessed | tf_op | source)
XLA Modules:
  0.0 451.5 jit_solution(1819920880127915274)
XLA Ops:
  8.7 18.2 %copy.64 = bf16[512,8,4,512]{3,1,2,0:T(8,128)(2,1)} copy(bf16[512,8,4,512]{3,2,1,0:T(4,128)(2,1)} %bitcast.365) | data formatting | bytes 33554432
  26.8 9.5 %copy.66 = bf16[512,8,4,512]{3,1,2,0:T(8,128)(2,1)} copy(bf16[512,8,4,512]{3,2,1,0:T(4,128)(2,1)S(1)} %bitcast.366) | data formatting | bytes 33554432
  36.4 8.4 %convolution_add_fusion.7 = f32[128,2048]{1,0:T(8,128)S(1)} fusion(bf16[4096,2048]{1,0:T(8,128)(2,1)} %bitcast.351, bf16[4,128,4096]{2,1,0:T(8,128)(2,1)} %param.6, s32[]{:T(128)S(6)} %min.22, pred[]{:T(512)S(6)} %eq.2, f32[2048]{0:T(1024)S(1)} %bitcast.368), kind=kOutput, calls=%fused_computation.13 | convolution fusion | flops 2148270080 | bytes 18882564 | tf_op jit(solution)/shard_map/dot_general | solution.py:49
  44.9 8.5 %convolution_add_fusion.6 = f32[128,2048]{1,0:T(8,128)S(1)} fusion(f32[128,2048]{1,0:T(8,128)S(1)} %convolution_add_fusion.7, bf16[4096,2048]{1,0:T(8,128)(2,1)} %bitcast.358, bf16[1,128,4096]{2,1,0:T(8,128)(2,1)} %all-gather.39.cloned.1.call-done), kind=kOutput, calls=%fused_computation.12 | convolution fusion | flops 2147745792 | bytes 19922944 | tf_op jit(solution)/shard_map/while/body/eval_jaxpr/dot_general | solution.py:33
  56.1 4.8 %collective-permute-start = (bf16[1,128,512]{2,1,0:T(8,128)(2,1)S(1)}, bf16[1,128,512]{2,1,0:T(8,128)(2,1)S(1)}, u32[]{:S(2)}, u32[]{:S(2)}) collective-permute-start(bf16[1,128,512]{2,1,0:T(8,128)(2,1)S(1)} %get-tuple-element.137), channel_id=1, source_target_pairs={{0,8},{8,16},{16,24},{1,9},{9,17},{17,25},{2,10},{10,18},{18,26},{... | collective-permute-start | bytes 393224 | tf_op jit(solution)/shard_map/ppermute | solution.py:10
  64.6 16.3 %all-gather.17.cloned.1.call-done = bf16[128,4096]{1,0:T(8,128)(2,1)} async-done(((bf16[128,512]{1,0:T(8,128)(2,1)}), bf16[128,4096]{1,0:T(8,128)(2,1)}) %all-gather.17.cloned.1.call-update) | async-done | bytes 1048592 | tf_op jit(solution)/shard_map/while/body/eval_jaxpr/all_gather | solution.py:39
  82.5 9.1 %fusion.159 = f32[128,2048]{1,0:T(8,128)} fusion(bf16[128,4096]{1,0:T(8,128)(2,1)S(1)} %bitcast_select_fusion, bf16[4096,2048]{1,0:T(8,128)(2,1)} %bitcast.359), kind=kOutput, calls=%fused_computation.241 | convolution fusion | flops 2147483648 | bytes 18874368 | tf_op jit(solution)/shard_map/while/body/eval_jaxpr/dot_general | solution.py:33
  91.6 13.3 %all-gather.15.cloned.1.call-done = bf16[1,128,4096]{2,1,0:T(8,128)(2,1)} async-done(((bf16[1,128,512]{2,1,0:T(8,128)(2,1)}), bf16[1,128,4096]{2,1,0:T(8,128)(2,1)}) %all-gather.15.cloned.1.call-update) | async-done | bytes 1048592 | tf_op jit(solution)/shard_map/all_gather | solution.py:65
  104.9 9.7 %fusion.5 = f32[128,2048]{1,0:T(8,128)} fusion(f32[128,2048]{1,0:T(8,128)} %fusion.159, bf16[4096,2048]{1,0:T(8,128)(2,1)} %bitcast.352, bf16[1,128,4096]{2,1,0:T(8,128)(2,1)} %all-gather.15.cloned.1.call-done, bf16[4,128,4096]{2,1,0:T(8,128)(2,1)} %param.6, s32[]{:T(128)S(6)} %min.23, pred[]{:T(512)S(6)} %eq.2, f32[2048]{0:T(1024)S(1)} %bitcast.369), kind=kOutput, calls=%fused_computation.11 | convolution fusion | flops 2148532224 | bytes 20979716 | tf_op jit(solution)/shard_map/dot_general | solution.py:49
  117.5 3.5 fusion.157
  122.4 3.7 collective-permute-start.1
  126.1 3.1 collective-permute-done.1
  130.2 14.4 %all-gather.21.cloned.1.call-done = bf16[128,4096]{1,0:T(8,128)(2,1)} async-done(((bf16[128,512]{1,0:T(8,128)(2,1)}), bf16[128,4096]{1,0:T(8,128)(2,1)}) %all-gather.21.cloned.1.call-update) | async-done | bytes 1048592 | tf_op jit(solution)/shard_map/while/body/eval_jaxpr/all_gather | solution.py:39
  144.6 9.5 %fusion.39 = f32[128,2048]{1,0:T(8,128)} fusion(bf16[4096,2048]{1,0:T(8,128)(2,1)} %bitcast.360, bf16[128,4096]{1,0:T(8,128)(2,1)} %all-gather.21.cloned.1.call-done, bf16[128,4096]{1,0:T(8,128)(2,1)S(1)} %bitcast_select_fusion, pred[]{:T(512)S(6)} %and.23), kind=kOutput, calls=%fused_computation.52 | convolution fusion | flops 2148007936 | bytes 19922944 | tf_op jit(solution)/shard_map/while/body/eval_jaxpr/dot_general | solution.py:33
  154.0 13.9 %all-gather.19.cloned.1.call-done = bf16[1,128,4096]{2,1,0:T(8,128)(2,1)} async-done(((bf16[1,128,512]{2,1,0:T(8,128)(2,1)}), bf16[1,128,4096]{2,1,0:T(8,128)(2,1)}) %all-gather.19.cloned.1.call-update) | async-done | bytes 1048592 | tf_op jit(solution)/shard_map/all_gather | solution.py:65
  167.9 9.7 %fusion.4 = f32[128,2048]{1,0:T(8,128)} fusion(f32[128,2048]{1,0:T(8,128)} %fusion.39, bf16[4096,2048]{1,0:T(8,128)(2,1)} %bitcast.353, bf16[1,128,4096]{2,1,0:T(8,128)(2,1)} %all-gather.19.cloned.1.call-done, bf16[4,128,4096]{2,1,0:T(8,128)(2,1)} %param.6, s32[]{:T(128)S(6)} %min.24, pred[]{:T(512)S(6)} %eq.2, f32[2048]{0:T(1024)S(1)} %bitcast.370), kind=kOutput, calls=%fused_computation.9 | convolution fusion | flops 2148532224 | bytes 20979716 | tf_op jit(solution)/shard_map/dot_general | solution.py:49
  177.6 2.9 reshape.903
  180.5 3.9 fusion.156
  189.2 3.7 collective-permute-start.2
  192.9 3.1 collective-permute-done.2
  197.0 12.5 %all-gather.25.cloned.1.call-done = bf16[128,4096]{1,0:T(8,128)(2,1)} async-done(((bf16[128,512]{1,0:T(8,128)(2,1)}), bf16[128,4096]{1,0:T(8,128)(2,1)}) %all-gather.25.cloned.1.call-update) | async-done | bytes 1048592 | tf_op jit(solution)/shard_map/while/body/eval_jaxpr/all_gather | solution.py:39
  211.1 9.1 %fusion.160 = f32[128,2048]{1,0:T(8,128)} fusion(bf16[128,4096]{1,0:T(8,128)(2,1)S(1)} %broadcast_select_fusion.2, bf16[4096,2048]{1,0:T(8,128)(2,1)} %bitcast.361), kind=kOutput, calls=%fused_computation.242 | convolution fusion | flops 2147483648 | bytes 18874368 | tf_op jit(solution)/shard_map/while/body/eval_jaxpr/dot_general | solution.py:33
  220.2 12.7 %all-gather.23.cloned.1.call-done = bf16[1,128,4096]{2,1,0:T(8,128)(2,1)} async-done(((bf16[1,128,512]{2,1,0:T(8,128)(2,1)}), bf16[1,128,4096]{2,1,0:T(8,128)(2,1)}) %all-gather.23.cloned.1.call-update) | async-done | bytes 1048592 | tf_op jit(solution)/shard_map/all_gather | solution.py:65
  232.9 9.7 %fusion.3 = f32[128,2048]{1,0:T(8,128)} fusion(f32[128,2048]{1,0:T(8,128)} %fusion.160, bf16[4096,2048]{1,0:T(8,128)(2,1)} %bitcast.354, bf16[1,128,4096]{2,1,0:T(8,128)(2,1)} %all-gather.23.cloned.1.call-done, bf16[4,128,4096]{2,1,0:T(8,128)(2,1)} %param.6, s32[]{:T(128)S(6)} %min.25, pred[]{:T(512)S(6)} %eq.2, f32[2048]{0:T(1024)S(1)} %bitcast.371), kind=kOutput, calls=%fused_computation.7 | convolution fusion | flops 2148532224 | bytes 20979716 | tf_op jit(solution)/shard_map/dot_general | solution.py:49
  242.6 2.9 reshape.905
  245.5 3.9 fusion.155
  253.0 3.7 collective-permute-start.3
  256.7 3.1 collective-permute-done.3
  261.0 13.0 %all-gather.29.cloned.1.call-done = bf16[128,4096]{1,0:T(8,128)(2,1)} async-done(((bf16[128,512]{1,0:T(8,128)(2,1)}), bf16[128,4096]{1,0:T(8,128)(2,1)}) %all-gather.29.cloned.1.call-update) | async-done | bytes 1048592 | tf_op jit(solution)/shard_map/while/body/eval_jaxpr/all_gather | solution.py:39
  274.0 9.5 %fusion.40 = f32[128,2048]{1,0:T(8,128)} fusion(bf16[4096,2048]{1,0:T(8,128)(2,1)} %bitcast.362, bf16[128,4096]{1,0:T(8,128)(2,1)} %all-gather.29.cloned.1.call-done, bf16[128,4096]{1,0:T(8,128)(2,1)S(1)} %broadcast_select_fusion.2, pred[]{:T(512)S(6)} %and.25), kind=kOutput, calls=%fused_computation.53 | convolution fusion | flops 2148007936 | bytes 19922944 | tf_op jit(solution)/shard_map/while/body/eval_jaxpr/dot_general | solution.py:33
  283.5 14.6 %all-gather.27.cloned.1.call-done = bf16[1,128,4096]{2,1,0:T(8,128)(2,1)} async-done(((bf16[1,128,512]{2,1,0:T(8,128)(2,1)}), bf16[1,128,4096]{2,1,0:T(8,128)(2,1)}) %all-gather.27.cloned.1.call-update) | async-done | bytes 1048592 | tf_op jit(solution)/shard_map/all_gather | solution.py:65
  298.1 9.7 %fusion.2 = f32[128,2048]{1,0:T(8,128)} fusion(f32[128,2048]{1,0:T(8,128)} %fusion.40, bf16[4096,2048]{1,0:T(8,128)(2,1)} %bitcast.355, bf16[1,128,4096]{2,1,0:T(8,128)(2,1)} %all-gather.27.cloned.1.call-done, bf16[4,128,4096]{2,1,0:T(8,128)(2,1)} %param.6, s32[]{:T(128)S(6)} %min.26, pred[]{:T(512)S(6)} %eq.2, f32[2048]{0:T(1024)S(1)} %bitcast.372), kind=kOutput, calls=%fused_computation.5 | convolution fusion | flops 2148532224 | bytes 20979716 | tf_op jit(solution)/shard_map/dot_general | solution.py:49
  307.8 2.9 reshape.907
  310.7 3.9 fusion.154
  319.4 3.7 collective-permute-start.4
  323.1 3.1 collective-permute-done.4
  327.1 12.5 %all-gather.33.cloned.1.call-done = bf16[128,4096]{1,0:T(8,128)(2,1)} async-done(((bf16[128,512]{1,0:T(8,128)(2,1)}), bf16[128,4096]{1,0:T(8,128)(2,1)}) %all-gather.33.cloned.1.call-update) | async-done | bytes 1048592 | tf_op jit(solution)/shard_map/while/body/eval_jaxpr/all_gather | solution.py:39
  341.0 9.1 %fusion.161 = f32[128,2048]{1,0:T(8,128)} fusion(bf16[128,4096]{1,0:T(8,128)(2,1)S(1)} %broadcast_select_fusion, bf16[4096,2048]{1,0:T(8,128)(2,1)} %bitcast.363), kind=kOutput, calls=%fused_computation.243 | convolution fusion | flops 2147483648 | bytes 18874368 | tf_op jit(solution)/shard_map/while/body/eval_jaxpr/dot_general | solution.py:33
  350.1 13.0 %all-gather.31.cloned.1.call-done = bf16[1,128,4096]{2,1,0:T(8,128)(2,1)} async-done(((bf16[1,128,512]{2,1,0:T(8,128)(2,1)}), bf16[1,128,4096]{2,1,0:T(8,128)(2,1)}) %all-gather.31.cloned.1.call-update) | async-done | bytes 1048592 | tf_op jit(solution)/shard_map/all_gather | solution.py:65
  363.1 9.7 %fusion.1 = f32[128,2048]{1,0:T(8,128)} fusion(f32[128,2048]{1,0:T(8,128)} %fusion.161, bf16[4096,2048]{1,0:T(8,128)(2,1)} %bitcast.356, bf16[1,128,4096]{2,1,0:T(8,128)(2,1)} %all-gather.31.cloned.1.call-done, bf16[4,128,4096]{2,1,0:T(8,128)(2,1)} %param.6, s32[]{:T(128)S(6)} %min.27, pred[]{:T(512)S(6)} %eq.2, f32[2048]{0:T(1024)S(1)} %bitcast.373), kind=kOutput, calls=%fused_computation.3 | convolution fusion | flops 2148532224 | bytes 20979716 | tf_op jit(solution)/shard_map/dot_general | solution.py:49
  372.8 2.9 reshape.909
  375.7 3.9 fusion.153
  383.9 3.9 collective-permute-start.5
  392.2 12.6 %all-gather.37.cloned.1.call-done = bf16[128,4096]{1,0:T(8,128)(2,1)} async-done(((bf16[128,512]{1,0:T(8,128)(2,1)}), bf16[128,4096]{1,0:T(8,128)(2,1)}) %all-gather.37.cloned.1.call-update) | async-done | bytes 1048592 | tf_op jit(solution)/shard_map/while/body/eval_jaxpr/all_gather | solution.py:39
  404.7 9.1 %fusion.14 = f32[128,2048]{1,0:T(8,128)} fusion(bf16[4096,2048]{1,0:T(8,128)(2,1)} %bitcast.364, bf16[128,4096]{1,0:T(8,128)(2,1)} %all-gather.37.cloned.1.call-done, bf16[128,4096]{1,0:T(8,128)(2,1)S(1)} %broadcast_select_fusion, pred[]{:T(512)S(6)} %and.27), kind=kOutput, calls=%fused_computation.23 | convolution fusion | flops 2148007936 | bytes 19922944 | tf_op jit(solution)/shard_map/while/body/eval_jaxpr/dot_general | solution.py:33
  413.9 14.9 %all-gather.35.cloned.1.call-done = bf16[1,128,4096]{2,1,0:T(8,128)(2,1)} async-done(((bf16[1,128,512]{2,1,0:T(8,128)(2,1)}), bf16[1,128,4096]{2,1,0:T(8,128)(2,1)}) %all-gather.35.cloned.1.call-update) | async-done | bytes 1048592 | tf_op jit(solution)/shard_map/all_gather | solution.py:65
  428.8 8.8 %fusion = f32[128,2048]{1,0:T(8,128)S(1)} fusion(f32[128,2048]{1,0:T(8,128)} %fusion.14, bf16[4096,2048]{1,0:T(8,128)(2,1)} %bitcast.357, bf16[1,128,4096]{2,1,0:T(8,128)(2,1)} %all-gather.35.cloned.1.call-done, bf16[4,128,4096]{2,1,0:T(8,128)(2,1)} %param.6, s32[]{:T(128)S(6)} %min.28, pred[]{:T(512)S(6)} %eq.2, f32[2048]{0:T(1024)S(1)} %bitcast.374), kind=kOutput, calls=%fused_computation.1 | convolution fusion | flops 2148532224 | bytes 20979716 | tf_op jit(solution)/shard_map/dot_general | solution.py:49
  439.2 3.6 fusion.152
  (107 shorter events, 45.8 us)
Async XLA Ops:
  7.2 37.7 %all-gather.39.cloned.1.call-start = ((), (), s32[]{:S(2)}) async-start(), calls=%async_computation.12 | async-start | bytes 1179648 | tf_op jit(solution)/shard_map/all_gather | solution.py:26
  7.9 73.0 %all-gather.17.cloned.1.call-start = ((), (), s32[]{:S(2)}) async-start(), calls=%async_computation.1 | async-start | bytes 1179648 | tf_op jit(solution)/shard_map/while/body/eval_jaxpr/all_gather | solution.py:39
  8.7 18.2 %copy-start = (bf16[1,4096,4,512]{3,2,1,0:T(4,128)(2,1)S(1)}, bf16[1,4096,4,512]{3,2,1,0:T(4,128)(2,1)}, u32[]{:S(2)}) copy-start(bf16[1,4096,4,512]{3,2,1,0:T(4,128)(2,1)} %param.8) | copy-start | bytes 50331652
  44.8 10.0 %copy-start.3 = (f32[1,128,512]{2,1,0:T(8,128)S(1)}, f32[1,128,512]{2,1,0:T(8,128)}, u32[]{:S(2)}) copy-start(f32[1,128,512]{2,1,0:T(8,128)} %param.11) | copy-start | bytes 786436
  55.8 49.1 %all-gather.15.cloned.1.call-start = ((), (), s32[]{:S(2)}) async-start(), calls=%async_computation | async-start | bytes 1179648 | tf_op jit(solution)/shard_map/all_gather | solution.py:65
  56.1 7.6 %collective-permute-start = (bf16[1,128,512]{2,1,0:T(8,128)(2,1)S(1)}, bf16[1,128,512]{2,1,0:T(8,128)(2,1)S(1)}, u32[]{:S(2)}, u32[]{:S(2)}) collective-permute-start(bf16[1,128,512]{2,1,0:T(8,128)(2,1)S(1)} %get-tuple-element.137), channel_id=1, source_target_pairs={{0,8},{8,16},{16,24},{1,9},{9,17},{17,25},{2,10},{10,18},{18,26},{... | collective-permute-start | bytes 393224 | tf_op jit(solution)/shard_map/ppermute | solution.py:10
  63.7 0.7 copy-start.23
  64.4 80.2 %all-gather.21.cloned.1.call-start = ((), (), s32[]{:S(2)}) async-start(), calls=%async_computation.3 | async-start | bytes 1179648 | tf_op jit(solution)/shard_map/while/body/eval_jaxpr/all_gather | solution.py:39
  122.0 65.2 %copy-start.4 = (f32[128,1,512]{2,0,1:T(8,128)}, f32[128,1,512]{2,0,1:T(8,128)S(1)}, u32[]{:S(2)}) copy-start(f32[128,1,512]{2,0,1:T(8,128)S(1)} %get-tuple-element.125) | copy-start | bytes 786436
  122.1 45.8 %all-gather.19.cloned.1.call-start = ((), (), s32[]{:S(2)}) async-start(), calls=%async_computation.2 | async-start | bytes 1179648 | tf_op jit(solution)/shard_map/all_gather | solution.py:65
  122.4 6.8 %collective-permute-start.1 = (bf16[1,128,512]{2,1,0:T(8,128)(2,1)S(1)}, bf16[1,128,512]{2,1,0:T(8,128)(2,1)S(1)}, u32[]{:S(2)}, u32[]{:S(2)}) collective-permute-start(bf16[1,128,512]{2,1,0:T(8,128)(2,1)S(1)} %get-tuple-element.133), channel_id=1, source_target_pairs={{0,8},{8,16},{16,24},{1,9},{9,17},{17,25},{2,10},{10,18},{18,26},{... | collective-permute-start | bytes 393224 | tf_op jit(solution)/shard_map/ppermute | solution.py:10
  129.2 0.6 copy-start.25
  129.9 79.6 %all-gather.25.cloned.1.call-start = ((), (), s32[]{:S(2)}) async-start(), calls=%async_computation.5 | async-start | bytes 1179648 | tf_op jit(solution)/shard_map/while/body/eval_jaxpr/all_gather | solution.py:39
  184.5 0.7 copy-start.18
  187.1 45.8 %all-gather.23.cloned.1.call-start = ((), (), s32[]{:S(2)}) async-start(), calls=%async_computation.4 | async-start | bytes 1179648 | tf_op jit(solution)/shard_map/all_gather | solution.py:65
  189.2 7.8 %copy-start.6 = (bf16[4,128,512]{2,1,0:T(8,128)(2,1)}, bf16[4,128,512]{2,1,0:T(8,128)(2,1)S(1)}, u32[]{:S(2)}) copy-start(bf16[4,128,512]{2,1,0:T(8,128)(2,1)S(1)} %get-tuple-element.120) | copy-start | bytes 1572868
  189.2 6.8 %collective-permute-start.2 = (bf16[1,128,512]{2,1,0:T(8,128)(2,1)S(1)}, bf16[1,128,512]{2,1,0:T(8,128)(2,1)S(1)}, u32[]{:S(2)}, u32[]{:S(2)}) collective-permute-start(bf16[1,128,512]{2,1,0:T(8,128)(2,1)S(1)} %get-tuple-element.121), channel_id=1, source_target_pairs={{0,8},{8,16},{16,24},{1,9},{9,17},{17,25},{2,10},{10,18},{18,26},{... | collective-permute-start | bytes 393224 | tf_op jit(solution)/shard_map/ppermute | solution.py:10
  196.0 0.6 copy-start.24
  196.7 77.3 %all-gather.29.cloned.1.call-start = ((), (), s32[]{:S(2)}) async-start(), calls=%async_computation.7 | async-start | bytes 1179648 | tf_op jit(solution)/shard_map/while/body/eval_jaxpr/all_gather | solution.py:39
  220.2 29.2 %copy-start.5 = (f32[128,1,512]{2,0,1:T(8,128)S(1)}, f32[128,1,512]{2,0,1:T(8,128)}, u32[]{:S(2)}) copy-start(f32[128,1,512]{2,0,1:T(8,128)} %copy-done.4) | copy-start | bytes 786436
  220.2 31.5 %copy-start.7 = (bf16[4,128,512]{2,1,0:T(8,128)(2,1)S(1)}, bf16[4,128,512]{2,1,0:T(8,128)(2,1)}, u32[]{:S(2)}) copy-start(bf16[4,128,512]{2,1,0:T(8,128)(2,1)} %copy-done.6) | copy-start | bytes 1572868
  220.2 31.5 %copy-start.14 = (f32[1,128,512]{2,1,0:T(8,128)S(1)}, f32[1,128,512]{2,1,0:T(8,128)}, u32[]{:S(2)}) copy-start(f32[1,128,512]{2,1,0:T(8,128)} %get-tuple-element.122) | copy-start | bytes 786436
  249.5 2.2 copy-start.20
  251.7 65.7 %copy-start.1 = (f32[128,1,512]{2,0,1:T(8,128)}, f32[128,1,512]{2,0,1:T(8,128)S(1)}, u32[]{:S(2)}) copy-start(f32[128,1,512]{2,0,1:T(8,128)S(1)} %get-tuple-element.109) | copy-start | bytes 786436
  251.7 46.4 %all-gather.27.cloned.1.call-start = ((), (), s32[]{:S(2)}) async-start(), calls=%async_computation.6 | async-start | bytes 1179648 | tf_op jit(solution)/shard_map/all_gather | solution.py:65
  253.0 6.8 %collective-permute-start.3 = (bf16[1,128,512]{2,1,0:T(8,128)(2,1)S(1)}, bf16[1,128,512]{2,1,0:T(8,128)(2,1)S(1)}, u32[]{:S(2)}, u32[]{:S(2)}) collective-permute-start(bf16[1,128,512]{2,1,0:T(8,128)(2,1)S(1)} %get-tuple-element.111), channel_id=1, source_target_pairs={{0,8},{8,16},{16,24},{1,9},{9,17},{17,25},{2,10},{10,18},{18,26},{... | collective-permute-start | bytes 393224 | tf_op jit(solution)/shard_map/ppermute | solution.py:10
  259.8 0.7 copy-start.26
  260.5 79.1 %all-gather.33.cloned.1.call-start = ((), (), s32[]{:S(2)}) async-start(), calls=%async_computation.9 | async-start | bytes 1179648 | tf_op jit(solution)/shard_map/while/body/eval_jaxpr/all_gather | solution.py:39
  283.5 33.9 %copy-start.15 = (f32[1,128,512]{2,1,0:T(8,128)S(1)}, f32[1,128,512]{2,1,0:T(8,128)}, u32[]{:S(2)}) copy-start(f32[1,128,512]{2,1,0:T(8,128)} %get-tuple-element.122) | copy-start | bytes 786436
  314.7 0.7 copy-start.17
  317.3 45.8 %all-gather.31.cloned.1.call-start = ((), (), s32[]{:S(2)}) async-start(), calls=%async_computation.8 | async-start | bytes 1179648 | tf_op jit(solution)/shard_map/all_gather | solution.py:65
  319.4 7.7 %copy-start.8 = (bf16[4,128,512]{2,1,0:T(8,128)(2,1)}, bf16[4,128,512]{2,1,0:T(8,128)(2,1)S(1)}, u32[]{:S(2)}) copy-start(bf16[4,128,512]{2,1,0:T(8,128)(2,1)S(1)} %get-tuple-element.98) | copy-start | bytes 1572868
  319.4 6.8 %collective-permute-start.4 = (bf16[1,128,512]{2,1,0:T(8,128)(2,1)S(1)}, bf16[1,128,512]{2,1,0:T(8,128)(2,1)S(1)}, u32[]{:S(2)}, u32[]{:S(2)}) collective-permute-start(bf16[1,128,512]{2,1,0:T(8,128)(2,1)S(1)} %get-tuple-element.99), channel_id=1, source_target_pairs={{0,8},{8,16},{16,24},{1,9},{9,17},{17,25},{2,10},{10,18},{18,26},{... | collective-permute-start | bytes 393224 | tf_op jit(solution)/shard_map/ppermute | solution.py:10
  326.2 0.7 copy-start.22
  326.9 77.8 %all-gather.37.cloned.1.call-start = ((), (), s32[]{:S(2)}) async-start(), calls=%async_computation.11 | async-start | bytes 1179648 | tf_op jit(solution)/shard_map/while/body/eval_jaxpr/all_gather | solution.py:39
  350.1 30.3 %copy-start.2 = (f32[128,1,512]{2,0,1:T(8,128)S(1)}, f32[128,1,512]{2,0,1:T(8,128)}, u32[]{:S(2)}) copy-start(f32[128,1,512]{2,0,1:T(8,128)} %copy-done.1) | copy-start | bytes 786436
  350.1 32.4 %copy-start.9 = (bf16[4,128,512]{2,1,0:T(8,128)(2,1)S(1)}, bf16[4,128,512]{2,1,0:T(8,128)(2,1)}, u32[]{:S(2)}) copy-start(bf16[4,128,512]{2,1,0:T(8,128)(2,1)} %copy-done.8) | copy-start | bytes 1572868
  379.7 0.7 copy-start.19
  379.7 34.2 %copy-start.10 = (f32[128,1,512]{2,1,0:T(1,128)}, f32[128,1,512]{2,1,0:T(1,128)S(1)}, u32[]{:S(2)}) copy-start(f32[128,1,512]{2,1,0:T(1,128)S(1)} %get-tuple-element.156) | copy-start | bytes 786436
  379.7 34.2 %copy-start.12 = (f32[128,1,512]{2,1,0:T(1,128)}, f32[128,1,512]{2,1,0:T(1,128)S(1)}, u32[]{:S(2)}) copy-start(f32[128,1,512]{2,1,0:T(1,128)S(1)} %get-tuple-element.157) | copy-start | bytes 786436
  382.4 46.4 %all-gather.35.cloned.1.call-start = ((), (), s32[]{:S(2)}) async-start(), calls=%async_computation.10 | async-start | bytes 1179648 | tf_op jit(solution)/shard_map/all_gather | solution.py:65
  383.9 6.8 %collective-permute-start.5 = (bf16[1,128,512]{2,1,0:T(8,128)(2,1)S(1)}, bf16[1,128,512]{2,1,0:T(8,128)(2,1)S(1)}, u32[]{:S(2)}, u32[]{:S(2)}) collective-permute-start(bf16[1,128,512]{2,1,0:T(8,128)(2,1)S(1)} %get-tuple-element.89), channel_id=1, source_target_pairs={{0,8},{8,16},{16,24},{1,9},{9,17},{17,25},{2,10},{10,18},{18,26},{... | collective-permute-start | bytes 393224 | tf_op jit(solution)/shard_map/ppermute | solution.py:10
  390.7 0.7 copy-start.21
  413.9 29.0 %copy-start.16 = (f32[1,128,512]{2,1,0:T(8,128)S(1)}, f32[1,128,512]{2,1,0:T(8,128)}, u32[]{:S(2)}) copy-start(f32[1,128,512]{2,1,0:T(8,128)} %get-tuple-element.100) | copy-start | bytes 786436
  428.8 14.1 %copy-start.11 = (f32[128,1,512]{2,1,0:T(1,128)S(1)}, f32[128,1,512]{2,1,0:T(1,128)}, u32[]{:S(2)}) copy-start(f32[128,1,512]{2,1,0:T(1,128)} %copy-done.10) | copy-start | bytes 786436
  428.8 14.1 %copy-start.13 = (f32[128,1,512]{2,1,0:T(1,128)S(1)}, f32[128,1,512]{2,1,0:T(1,128)}, u32[]{:S(2)}) copy-start(f32[128,1,512]{2,1,0:T(1,128)} %copy-done.12) | copy-start | bytes 786436
Sparse Core Ops, SparseCore 0:
  9.6 24.9 all-gather.38
  55.9 24.8 all-gather.16
  83.0 21.8 all-gather.14
  122.2 22.3 all-gather.20
  146.0 21.8 all-gather.18
  187.3 22.1 all-gather.24
  211.1 21.8 all-gather.22
  251.8 22.1 all-gather.28
  276.2 21.8 all-gather.26
  317.4 22.1 all-gather.32
  341.3 21.8 all-gather.30
  382.5 22.1 all-gather.36
  406.9 21.8 all-gather.34
where the time goes:
time: 459 us; the launch traced here: 452 us
  waiting for transfers between devices  183 us (40%)
  matrix products  129 us (28%)
  local copies, waits for them, and re-layouts  75.9 us (17%)
  starting transfers between devices  25.3 us (6%)
  other arithmetic  23.8 us (5%)
  between operations  14.6 us (3%)
    all_gather x6, waiting for transfers between devices, body(): arrived = lax.all_gather(received, 'col', axis=2, tiled=True)  82.4 us
    all_gather x6, waiting for transfers between devices, advance(): hidden_wide = lax.all_gather(hidden_new, 'col', axis=1, tiled=True)  81.2 us
    dot_general x7, matrix products, body(): jnp.dot(source.reshape(span * batch, width), weight_in, preferred_element...  65.6 us
    dot_general x7, matrix products, advance(): jnp.dot(hidden_prev, weight_rec, preferred_element_type=jnp.float32)  63.8 us
    unnamed x58, local copies, waits for them, and re-layouts  35.2 us
    ppermute x6, starting transfers between devices, passed_along(): lax.ppermute(value, axis, [(source, source + steps) for source in range(f...  23.5 us
    ppermute x6, waiting for transfers between devices, passed_along(): lax.ppermute(value, axis, [(source, source + steps) for source in range(f...  18.1 us
    reshape x7, local copies, waits for them, and re-layouts, advance(): gates = gates.reshape(batch, 4, local)  17 us
  transfers between devices with their start and end apart: 19, of which 18 were waited for; matrix products, arithmetic and copies ran while one was open for 23% of the time, Pallas kernels for 0%

commit v1 on v0

--- a/solution.py
+++ b/solution.py
@@ -36,7 +36,14 @@
             gates[:, 2]
         )
         hidden_new = (jax.nn.sigmoid(gates[:, 3]) * jnp.tanh(cell_new)).astype(jnp.bfloat16)
-        hidden_wide = lax.all_gather(hidden_new, "col", axis=1, tiled=True)
+        devices = lax.axis_size("col")
+        forward = [(i, (i + 1) % devices) for i in range(devices)]
+        parts = [hidden_new]
+        for reach in range(1, devices):
+            parts = [lax.ppermute(parts[0], "col", forward), *parts]
+        result = jnp.concatenate(parts, axis=1)
+        shift = (lax.axis_index("col") + 1) * parts[-1].shape[1]
+        hidden_wide = jnp.roll(result, shift, axis=1)
         return ((hidden_wide, cell_new), (hidden_new, hidden_wide))
 
     for turn in range(rounds):

time: 459 us -> 552 us (1.20)
  waiting for transfers between devices: 183 us -> 262 us
  local copies, waits for them, and re-layouts: 75.9 us -> 89.2 us
    ppermute x0 -> x42, waiting for transfers between devices: none -> 220 us  [advance(): parts = [lax.ppermute(parts[0], 'col', forward), *parts]]
    all_gather x6 -> x0, waiting for transfers between devices: 81.2 us -> none  [advance(): hidden_wide = lax.all_gather(hidden_new, 'col', axis=1, tiled=True)]
    all_gather x6, waiting for transfers between devices: 82.4 us -> 34.8 us  [body(): arrived = lax.all_gather(received, 'col', axis=2, tiled=True)]
    unnamed x58 -> x110, local copies, waits for them, and re-layouts: 35.2 us -> 53.6 us
    ppermute x6, waiting for transfers between devices: 18.1 us -> 5.97 us  [passed_along(): lax.ppermute(value, axis, [(source, source + steps) for source in range(f...]
  transfers between devices with their start and end apart: 19 -> 55, of which waited for: 18 -> 52; matrix products, arithmetic and copies ran while one was open for 23% -> 22% of each run, Pallas kernels for 0% -> 0%
where the time goes in v1:
time: 552 us; the launch traced here: 544 us
  waiting for transfers between devices  262 us (47%)
  matrix products  129 us (23%)
  local copies, waits for them, and re-layouts  89.2 us (16%)
  starting transfers between devices  26.7 us (5%)
  other arithmetic  22.2 us (4%)
  between operations  15.4 us (3%)
    ppermute x42, waiting for transfers between devices, advance(): parts = [lax.ppermute(parts[0], 'col', forward), *parts]  220 us
    dot_general x7, matrix products, body(): jnp.dot(source.reshape(span * batch, width), weight_in, preferred_element...  65.3 us
    dot_general x7, matrix products, advance(): jnp.dot(hidden_prev, weight_rec, preferred_element_type=jnp.float32)  63.3 us
    unnamed x110, local copies, waits for them, and re-layouts  53.6 us
    all_gather x6, waiting for transfers between devices, body(): arrived = lax.all_gather(received, 'col', axis=2, tiled=True)  34.8 us
    ppermute x6, starting transfers between devices, passed_along(): lax.ppermute(value, axis, [(source, source + steps) for source in range(f...  23 us
    reshape x7, local copies, waits for them, and re-layouts, advance(): gates = gates.reshape(batch, 4, local)  16 us
    slice x5, local copies, waits for them, and re-layouts, advance(): gates[:, 0]  15.2 us
  transfers between devices with their start and end apart: 55, of which 52 were waited for; matrix products, arithmetic and copies ran while one was open for 22% of the time, Pallas kernels for 0%

profile of v1, /device:TPU:0, one launch (start us, length us, event | category | flops | bytes accessed | tf_op | source)
XLA Modules:
  0.0 544.0 jit_solution(10443811419673792942)
XLA Ops:
  8.0 18.1 %copy.64 = bf16[512,8,4,512]{3,1,2,0:T(8,128)(2,1)} copy(bf16[512,8,4,512]{3,2,1,0:T(4,128)(2,1)} %bitcast.367) | data formatting | bytes 33554432
  26.1 9.4 %copy.66 = bf16[512,8,4,512]{3,1,2,0:T(8,128)(2,1)} copy(bf16[512,8,4,512]{3,2,1,0:T(4,128)(2,1)S(1)} %bitcast.368) | data formatting | bytes 33554432
  35.5 8.4 %convolution_add_fusion.7 = f32[128,2048]{1,0:T(8,128)S(1)} fusion(bf16[4096,2048]{1,0:T(8,128)(2,1)} %bitcast.353, bf16[4,128,4096]{2,1,0:T(8,128)(2,1)} %param.8, s32[]{:T(128)S(6)} %min.22, pred[]{:T(512)S(6)} %eq.4, f32[2048]{0:T(1024)S(1)} %bitcast.370), kind=kOutput, calls=%fused_computation.13 | convolution fusion | flops 2148270080 | bytes 18882564 | tf_op jit(solution)/shard_map/dot_general | solution.py:56
  44.0 8.5 %convolution_add_fusion.6 = f32[128,2048]{1,0:T(8,128)S(1)} fusion(f32[128,2048]{1,0:T(8,128)S(1)} %convolution_add_fusion.7, bf16[4096,2048]{1,0:T(8,128)(2,1)} %bitcast.360, bf16[1,128,4096]{2,1,0:T(8,128)(2,1)} %all-gather.21.cloned.1.call-done), kind=kOutput, calls=%fused_computation.12 | convolution fusion | flops 2147745792 | bytes 19922944 | tf_op jit(solution)/shard_map/while/body/eval_jaxpr/dot_general | solution.py:33
  54.9 6.7 %collective-permute-done.1 = bf16[128,512]{1,0:T(8,128)(2,1)S(1)} collective-permute-done((bf16[128,512]{1,0:T(8,128)(2,1)S(1)}, bf16[128,512]{1,0:T(8,128)(2,1)S(1)}, u32[]{:S(2)}, u32[]{:S(2)}) %collective-permute-start.1) | collective-permute-done | bytes 131104 | tf_op jit(solution)/shard_map/while/body/eval_jaxpr/ppermute | solution.py:43
  61.6 6.2 %collective-permute-done.2 = bf16[128,512]{1,0:T(8,128)(2,1)S(1)} collective-permute-done((bf16[128,512]{1,0:T(8,128)(2,1)S(1)}, bf16[128,512]{1,0:T(8,128)(2,1)S(1)}, u32[]{:S(2)}, u32[]{:S(2)}) %collective-permute-start.2) | collective-permute-done | bytes 131104 | tf_op jit(solution)/shard_map/while/body/eval_jaxpr/ppermute | solution.py:43
  67.8 6.2 %collective-permute-done.3 = bf16[128,512]{1,0:T(8,128)(2,1)S(1)} collective-permute-done((bf16[128,512]{1,0:T(8,128)(2,1)S(1)}, bf16[128,512]{1,0:T(8,128)(2,1)S(1)}, u32[]{:S(2)}, u32[]{:S(2)}) %collective-permute-start.3) | collective-permute-done | bytes 131104 | tf_op jit(solution)/shard_map/while/body/eval_jaxpr/ppermute | solution.py:43
  74.0 6.2 %collective-permute-done.4 = bf16[128,512]{1,0:T(8,128)(2,1)S(1)} collective-permute-done((bf16[128,512]{1,0:T(8,128)(2,1)S(1)}, bf16[128,512]{1,0:T(8,128)(2,1)S(1)}, u32[]{:S(2)}, u32[]{:S(2)}) %collective-permute-start.4) | collective-permute-done | bytes 131104 | tf_op jit(solution)/shard_map/while/body/eval_jaxpr/ppermute | solution.py:43
  80.2 6.2 %collective-permute-done.5 = bf16[128,512]{1,0:T(8,128)(2,1)S(1)} collective-permute-done((bf16[128,512]{1,0:T(8,128)(2,1)S(1)}, bf16[128,512]{1,0:T(8,128)(2,1)S(1)}, u32[]{:S(2)}, u32[]{:S(2)}) %collective-permute-start.5) | collective-permute-done | bytes 131104 | tf_op jit(solution)/shard_map/while/body/eval_jaxpr/ppermute | solution.py:43
  100.8 9.3 %fusion.171 = f32[128,2048]{1,0:T(8,128)} fusion(bf16[128,4096]{1,0:T(8,128)(2,1)S(1)} %fusion.19, bf16[4096,2048]{1,0:T(8,128)(2,1)} %bitcast.361), kind=kOutput, calls=%fused_computation.307 | convolution fusion | flops 2147483648 | bytes 18874368 | tf_op jit(solution)/shard_map/while/body/eval_jaxpr/dot_general | solution.py:33
  110.1 7.2 %all-gather.9.cloned.1.call-done = bf16[1,128,4096]{2,1,0:T(8,128)(2,1)} async-done(((bf16[1,128,512]{2,1,0:T(8,128)(2,1)}), bf16[1,128,4096]{2,1,0:T(8,128)(2,1)}) %all-gather.9.cloned.1.call-update) | async-done | bytes 1048592 | tf_op jit(solution)/shard_map/all_gather | solution.py:72
  117.3 9.7 %fusion.5 = f32[128,2048]{1,0:T(8,128)} fusion(f32[128,2048]{1,0:T(8,128)} %fusion.171, bf16[4096,2048]{1,0:T(8,128)(2,1)} %bitcast.354, bf16[1,128,4096]{2,1,0:T(8,128)(2,1)} %all-gather.9.cloned.1.call-done, bf16[4,128,4096]{2,1,0:T(8,128)(2,1)} %param.8, s32[]{:T(128)S(6)} %min.23, pred[]{:T(512)S(6)} %eq.4, f32[2048]{0:T(1024)S(1)} %bitcast.371), kind=kOutput, calls=%fused_computation.11 | convolution fusion | flops 2148532224 | bytes 20979716 | tf_op jit(solution)/shard_map/dot_general | solution.py:56
  140.8 6.2 %collective-permute-done.10 = bf16[128,512]{1,0:T(8,128)(2,1)S(1)} collective-permute-done((bf16[128,512]{1,0:T(8,128)(2,1)S(1)}, bf16[128,512]{1,0:T(8,128)(2,1)S(1)}, u32[]{:S(2)}, u32[]{:S(2)}) %collective-permute-start.10) | collective-permute-done | bytes 131104 | tf_op jit(solution)/shard_map/while/body/eval_jaxpr/ppermute | solution.py:43
  146.9 6.2 %collective-permute-done.11 = bf16[128,512]{1,0:T(8,128)(2,1)S(1)} collective-permute-done((bf16[128,512]{1,0:T(8,128)(2,1)S(1)}, bf16[128,512]{1,0:T(8,128)(2,1)S(1)}, u32[]{:S(2)}, u32[]{:S(2)}) %collective-permute-start.11) | collective-permute-done | bytes 131104 | tf_op jit(solution)/shard_map/while/body/eval_jaxpr/ppermute | solution.py:43
  153.8 6.3 %collective-permute-done.12 = bf16[128,512]{1,0:T(8,128)(2,1)} collective-permute-done((bf16[128,512]{1,0:T(8,128)(2,1)S(1)}, bf16[128,512]{1,0:T(8,128)(2,1)}, u32[]{:S(2)}, u32[]{:S(2)}) %collective-permute-start.12) | collective-permute-done | bytes 131104 | tf_op jit(solution)/shard_map/while/body/eval_jaxpr/ppermute | solution.py:43
  160.1 6.5 %collective-permute-done.13 = bf16[128,512]{1,0:T(8,128)(2,1)} collective-permute-done((bf16[128,512]{1,0:T(8,128)(2,1)}, bf16[128,512]{1,0:T(8,128)(2,1)}, u32[]{:S(2)}, u32[]{:S(2)}) %collective-permute-start.13) | collective-permute-done | bytes 131104 | tf_op jit(solution)/shard_map/while/body/eval_jaxpr/ppermute | solution.py:43
  184.8 8.2 %fusion.172 = f32[128,2048]{1,0:T(8,128)S(1)} fusion(bf16[128,4096]{1,0:T(8,128)(2,1)S(1)} %fusion.17, bf16[4096,2048]{1,0:T(8,128)(2,1)} %bitcast.362), kind=kOutput, calls=%fused_computation.308 | convolution fusion | flops 2147483648 | bytes 18874368 | tf_op jit(solution)/shard_map/while/body/eval_jaxpr/dot_general | solution.py:33
  197.6 9.5 %fusion.4 = f32[128,2048]{1,0:T(8,128)} fusion(f32[128,2048]{1,0:T(8,128)S(1)} %fusion.172, bf16[4096,2048]{1,0:T(8,128)(2,1)} %bitcast.355, bf16[1,128,4096]{2,1,0:T(8,128)(2,1)} %all-gather.11.cloned.1.call-done, bf16[4,128,4096]{2,1,0:T(8,128)(2,1)} %param.8, s32[]{:T(128)S(6)} %min.24, pred[]{:T(512)S(6)} %eq.4, f32[2048]{0:T(1024)S(1)} %bitcast.372), kind=kOutput, calls=%fused_computation.9 | convolution fusion | flops 2148532224 | bytes 20979716 | tf_op jit(solution)/shard_map/dot_general | solution.py:56
  215.3 6.0 %collective-permute-done.17 = bf16[128,512]{1,0:T(8,128)(2,1)S(1)} collective-permute-done((bf16[128,512]{1,0:T(8,128)(2,1)S(1)}, bf16[128,512]{1,0:T(8,128)(2,1)S(1)}, u32[]{:S(2)}, u32[]{:S(2)}) %collective-permute-start.17) | collective-permute-done | bytes 131104 | tf_op jit(solution)/shard_map/while/body/eval_jaxpr/ppermute | solution.py:43
  221.3 6.2 %collective-permute-done.18 = bf16[128,512]{1,0:T(8,128)(2,1)S(1)} collective-permute-done((bf16[128,512]{1,0:T(8,128)(2,1)S(1)}, bf16[128,512]{1,0:T(8,128)(2,1)S(1)}, u32[]{:S(2)}, u32[]{:S(2)}) %collective-permute-start.18) | collective-permute-done | bytes 131104 | tf_op jit(solution)/shard_map/while/body/eval_jaxpr/ppermute | solution.py:43
  227.5 6.2 %collective-permute-done.19 = bf16[128,512]{1,0:T(8,128)(2,1)S(1)} collective-permute-done((bf16[128,512]{1,0:T(8,128)(2,1)S(1)}, bf16[128,512]{1,0:T(8,128)(2,1)S(1)}, u32[]{:S(2)}, u32[]{:S(2)}) %collective-permute-start.19) | collective-permute-done | bytes 131104 | tf_op jit(solution)/shard_map/while/body/eval_jaxpr/ppermute | solution.py:43
  233.7 6.2 %collective-permute-done.20 = bf16[128,512]{1,0:T(8,128)(2,1)S(1)} collective-permute-done((bf16[128,512]{1,0:T(8,128)(2,1)S(1)}, bf16[128,512]{1,0:T(8,128)(2,1)S(1)}, u32[]{:S(2)}, u32[]{:S(2)}) %collective-permute-start.20) | collective-permute-done | bytes 131104 | tf_op jit(solution)/shard_map/while/body/eval_jaxpr/ppermute | solution.py:43
  239.9 6.3 %collective-permute-done.21 = bf16[128,512]{1,0:T(8,128)(2,1)} collective-permute-done((bf16[128,512]{1,0:T(8,128)(2,1)S(1)}, bf16[128,512]{1,0:T(8,128)(2,1)}, u32[]{:S(2)}, u32[]{:S(2)}) %collective-permute-start.21) | collective-permute-done | bytes 131104 | tf_op jit(solution)/shard_map/while/body/eval_jaxpr/ppermute | solution.py:43
  262.6 9.3 %fusion.173 = f32[128,2048]{1,0:T(8,128)} fusion(bf16[128,4096]{1,0:T(8,128)(2,1)S(1)} %fusion.15, bf16[4096,2048]{1,0:T(8,128)(2,1)} %bitcast.363), kind=kOutput, calls=%fused_computation.309 | convolution fusion | flops 2147483648 | bytes 18874368 | tf_op jit(solution)/shard_map/while/body/eval_jaxpr/dot_general | solution.py:33
  271.8 6.7 %all-gather.13.cloned.1.call-done = bf16[1,128,4096]{2,1,0:T(8,128)(2,1)} async-done(((bf16[1,128,512]{2,1,0:T(8,128)(2,1)}), bf16[1,128,4096]{2,1,0:T(8,128)(2,1)}) %all-gather.13.cloned.1.call-update) | async-done | bytes 1048592 | tf_op jit(solution)/shard_map/all_gather | solution.py:72
  278.5 9.7 %fusion.3 = f32[128,2048]{1,0:T(8,128)} fusion(f32[128,2048]{1,0:T(8,128)} %fusion.173, bf16[4096,2048]{1,0:T(8,128)(2,1)} %bitcast.356, bf16[1,128,4096]{2,1,0:T(8,128)(2,1)} %all-gather.13.cloned.1.call-done, bf16[4,128,4096]{2,1,0:T(8,128)(2,1)} %param.8, s32[]{:T(128)S(6)} %min.25, pred[]{:T(512)S(6)} %eq.4, f32[2048]{0:T(1024)S(1)} %bitcast.373), kind=kOutput, calls=%fused_computation.7 | convolution fusion | flops 2148532224 | bytes 20979716 | tf_op jit(solution)/shard_map/dot_general | solution.py:56
  296.1 6.0 %collective-permute-done.25 = bf16[128,512]{1,0:T(8,128)(2,1)S(1)} collective-permute-done((bf16[128,512]{1,0:T(8,128)(2,1)S(1)}, bf16[128,512]{1,0:T(8,128)(2,1)S(1)}, u32[]{:S(2)}, u32[]{:S(2)}) %collective-permute-start.25) | collective-permute-done | bytes 131104 | tf_op jit(solution)/shard_map/while/body/eval_jaxpr/ppermute | solution.py:43
  302.0 6.2 %collective-permute-done.26 = bf16[128,512]{1,0:T(8,128)(2,1)S(1)} collective-permute-done((bf16[128,512]{1,0:T(8,128)(2,1)S(1)}, bf16[128,512]{1,0:T(8,128)(2,1)S(1)}, u32[]{:S(2)}, u32[]{:S(2)}) %collective-permute-start.26) | collective-permute-done | bytes 131104 | tf_op jit(solution)/shard_map/while/body/eval_jaxpr/ppermute | solution.py:43
  308.2 6.2 %collective-permute-done.27 = bf16[128,512]{1,0:T(8,128)(2,1)S(1)} collective-permute-done((bf16[128,512]{1,0:T(8,128)(2,1)S(1)}, bf16[128,512]{1,0:T(8,128)(2,1)S(1)}, u32[]{:S(2)}, u32[]{:S(2)}) %collective-permute-start.27) | collective-permute-done | bytes 131104 | tf_op jit(solution)/shard_map/while/body/eval_jaxpr/ppermute | solution.py:43
  314.4 6.2 %collective-permute-done.28 = bf16[128,512]{1,0:T(8,128)(2,1)S(1)} collective-permute-done((bf16[128,512]{1,0:T(8,128)(2,1)S(1)}, bf16[128,512]{1,0:T(8,128)(2,1)S(1)}, u32[]{:S(2)}, u32[]{:S(2)}) %collective-permute-start.28) | collective-permute-done | bytes 131104 | tf_op jit(solution)/shard_map/while/body/eval_jaxpr/ppermute | solution.py:43
  320.6 6.2 %collective-permute-done.29 = bf16[128,512]{1,0:T(8,128)(2,1)S(1)} collective-permute-done((bf16[128,512]{1,0:T(8,128)(2,1)S(1)}, bf16[128,512]{1,0:T(8,128)(2,1)S(1)}, u32[]{:S(2)}, u32[]{:S(2)}) %collective-permute-start.29) | collective-permute-done | bytes 131104 | tf_op jit(solution)/shard_map/while/body/eval_jaxpr/ppermute | solution.py:43
  341.2 9.3 %fusion.174 = f32[128,2048]{1,0:T(8,128)} fusion(bf16[128,4096]{1,0:T(8,128)(2,1)S(1)} %fusion.13, bf16[4096,2048]{1,0:T(8,128)(2,1)} %bitcast.364), kind=kOutput, calls=%fused_computation.310 | convolution fusion | flops 2147483648 | bytes 18874368 | tf_op jit(solution)/shard_map/while/body/eval_jaxpr/dot_general | solution.py:33
  350.5 8.3 %all-gather.15.cloned.1.call-done = bf16[1,128,4096]{2,1,0:T(8,128)(2,1)} async-done(((bf16[1,128,512]{2,1,0:T(8,128)(2,1)}), bf16[1,128,4096]{2,1,0:T(8,128)(2,1)}) %all-gather.15.cloned.1.call-update) | async-done | bytes 1048592 | tf_op jit(solution)/shard_map/all_gather | solution.py:72
  358.9 9.7 %fusion.2 = f32[128,2048]{1,0:T(8,128)} fusion(f32[128,2048]{1,0:T(8,128)} %fusion.174, bf16[4096,2048]{1,0:T(8,128)(2,1)} %bitcast.357, bf16[1,128,4096]{2,1,0:T(8,128)(2,1)} %all-gather.15.cloned.1.call-done, bf16[4,128,4096]{2,1,0:T(8,128)(2,1)} %param.8, s32[]{:T(128)S(6)} %min.26, pred[]{:T(512)S(6)} %eq.4, f32[2048]{0:T(1024)S(1)} %bitcast.374), kind=kOutput, calls=%fused_computation.5 | convolution fusion | flops 2148532224 | bytes 20979716 | tf_op jit(solution)/shard_map/dot_general | solution.py:56
  377.3 6.0 %collective-permute-done.33 = bf16[128,512]{1,0:T(8,128)(2,1)S(1)} collective-permute-done((bf16[128,512]{1,0:T(8,128)(2,1)S(1)}, bf16[128,512]{1,0:T(8,128)(2,1)S(1)}, u32[]{:S(2)}, u32[]{:S(2)}) %collective-permute-start.33) | collective-permute-done | bytes 131104 | tf_op jit(solution)/shard_map/while/body/eval_jaxpr/ppermute | solution.py:43
  384.0 6.2 %collective-permute-done.34 = bf16[128,512]{1,0:T(8,128)(2,1)S(1)} collective-permute-done((bf16[128,512]{1,0:T(8,128)(2,1)S(1)}, bf16[128,512]{1,0:T(8,128)(2,1)S(1)}, u32[]{:S(2)}, u32[]{:S(2)}) %collective-permute-start.34) | collective-permute-done | bytes 131104 | tf_op jit(solution)/shard_map/while/body/eval_jaxpr/ppermute | solution.py:43
  390.8 6.2 %collective-permute-done.35 = bf16[128,512]{1,0:T(8,128)(2,1)S(1)} collective-permute-done((bf16[128,512]{1,0:T(8,128)(2,1)S(1)}, bf16[128,512]{1,0:T(8,128)(2,1)S(1)}, u32[]{:S(2)}, u32[]{:S(2)}) %collective-permute-start.35) | collective-permute-done | bytes 131104 | tf_op jit(solution)/shard_map/while/body/eval_jaxpr/ppermute | solution.py:43
  397.7 6.3 %collective-permute-done.36 = bf16[128,512]{1,0:T(8,128)(2,1)} collective-permute-done((bf16[128,512]{1,0:T(8,128)(2,1)S(1)}, bf16[128,512]{1,0:T(8,128)(2,1)}, u32[]{:S(2)}, u32[]{:S(2)}) %collective-permute-start.36) | collective-permute-done | bytes 131104 | tf_op jit(solution)/shard_map/while/body/eval_jaxpr/ppermute | solution.py:43
  404.0 6.5 %collective-permute-done.37 = bf16[128,512]{1,0:T(8,128)(2,1)} collective-permute-done((bf16[128,512]{1,0:T(8,128)(2,1)}, bf16[128,512]{1,0:T(8,128)(2,1)}, u32[]{:S(2)}, u32[]{:S(2)}) %collective-permute-start.37) | collective-permute-done | bytes 131104 | tf_op jit(solution)/shard_map/while/body/eval_jaxpr/ppermute | solution.py:43
  430.6 9.2 %fusion.175 = f32[128,2048]{1,0:T(8,128)} fusion(bf16[128,4096]{1,0:T(8,128)(2,1)S(1)} %fusion.11, bf16[4096,2048]{1,0:T(8,128)(2,1)} %bitcast.365), kind=kOutput, calls=%fused_computation.311 | convolution fusion | flops 2147483648 | bytes 18874368 | tf_op jit(solution)/shard_map/while/body/eval_jaxpr/dot_general | solution.py:33
  442.9 9.7 %fusion.1 = f32[128,2048]{1,0:T(8,128)} fusion(f32[128,2048]{1,0:T(8,128)} %fusion.175, bf16[4096,2048]{1,0:T(8,128)(2,1)} %bitcast.358, bf16[1,128,4096]{2,1,0:T(8,128)(2,1)} %all-gather.17.cloned.1.call-done, bf16[4,128,4096]{2,1,0:T(8,128)(2,1)} %param.8, s32[]{:T(128)S(6)} %min.27, pred[]{:T(512)S(6)} %eq.4, f32[2048]{0:T(1024)S(1)} %bitcast.375), kind=kOutput, calls=%fused_computation.3 | convolution fusion | flops 2148532224 | bytes 20979716 | tf_op jit(solution)/shard_map/dot_general | solution.py:56
  461.1 6.0 %collective-permute-done.41 = bf16[128,512]{1,0:T(8,128)(2,1)S(1)} collective-permute-done((bf16[128,512]{1,0:T(8,128)(2,1)S(1)}, bf16[128,512]{1,0:T(8,128)(2,1)S(1)}, u32[]{:S(2)}, u32[]{:S(2)}) %collective-permute-start.41) | collective-permute-done | bytes 131104 | tf_op jit(solution)/shard_map/while/body/eval_jaxpr/ppermute | solution.py:43
  467.1 6.2 %collective-permute-done.42 = bf16[128,512]{1,0:T(8,128)(2,1)S(1)} collective-permute-done((bf16[128,512]{1,0:T(8,128)(2,1)S(1)}, bf16[128,512]{1,0:T(8,128)(2,1)S(1)}, u32[]{:S(2)}, u32[]{:S(2)}) %collective-permute-start.42) | collective-permute-done | bytes 131104 | tf_op jit(solution)/shard_map/while/body/eval_jaxpr/ppermute | solution.py:43
  473.3 6.2 %collective-permute-done.43 = bf16[128,512]{1,0:T(8,128)(2,1)S(1)} collective-permute-done((bf16[128,512]{1,0:T(8,128)(2,1)S(1)}, bf16[128,512]{1,0:T(8,128)(2,1)S(1)}, u32[]{:S(2)}, u32[]{:S(2)}) %collective-permute-start.43) | collective-permute-done | bytes 131104 | tf_op jit(solution)/shard_map/while/body/eval_jaxpr/ppermute | solution.py:43
  479.4 6.2 %collective-permute-done.44 = bf16[128,512]{1,0:T(8,128)(2,1)S(1)} collective-permute-done((bf16[128,512]{1,0:T(8,128)(2,1)S(1)}, bf16[128,512]{1,0:T(8,128)(2,1)S(1)}, u32[]{:S(2)}, u32[]{:S(2)}) %collective-permute-start.44) | collective-permute-done | bytes 131104 | tf_op jit(solution)/shard_map/while/body/eval_jaxpr/ppermute | solution.py:43
  485.6 6.3 %collective-permute-done.45 = bf16[128,512]{1,0:T(8,128)(2,1)} collective-permute-done((bf16[128,512]{1,0:T(8,128)(2,1)S(1)}, bf16[128,512]{1,0:T(8,128)(2,1)}, u32[]{:S(2)}, u32[]{:S(2)}) %collective-permute-start.45) | collective-permute-done | bytes 131104 | tf_op jit(solution)/shard_map/while/body/eval_jaxpr/ppermute | solution.py:43
  509.0 9.5 %fusion.8 = f32[128,2048]{1,0:T(8,128)} fusion(bf16[4096,2048]{1,0:T(8,128)(2,1)} %bitcast.366, bf16[128,4096]{1,0:T(8,128)(2,1)S(1)} %copy-done.9, s32[]{:T(128)S(6)} %select_n.320, bf16[128,4096]{1,0:T(8,128)(2,1)S(1)} %constant_dynamic-update-slice_fusion.40, pred[]{:T(512)S(6)} %and.33), kind=kOutput, calls=%fused_computation.28 | convolution fusion | flops 2150105088 | bytes 19922948 | tf_op jit(solution)/shard_map/while/body/eval_jaxpr/dot_general | solution.py:33
  523.4 8.7 %fusion = f32[128,2048]{1,0:T(8,128)S(1)} fusion(f32[128,2048]{1,0:T(8,128)} %fusion.8, bf16[4096,2048]{1,0:T(8,128)(2,1)} %bitcast.359, bf16[1,128,4096]{2,1,0:T(8,128)(2,1)} %all-gather.19.cloned.1.call-done, bf16[4,128,4096]{2,1,0:T(8,128)(2,1)} %param.8, s32[]{:T(128)S(6)} %min.28, pred[]{:T(512)S(6)} %eq.4, f32[2048]{0:T(1024)S(1)} %bitcast.376), kind=kOutput, calls=%fused_computation.1 | convolution fusion | flops 2148532224 | bytes 20979716 | tf_op jit(solution)/shard_map/dot_general | solution.py:56
  (233 shorter events, 170.1 us)
Async XLA Ops:
  7.2 36.8 %all-gather.21.cloned.1.call-start = ((), (), s32[]{:S(2)}) async-start(), calls=%async_computation.6 | async-start | bytes 1179648 | tf_op jit(solution)/shard_map/all_gather | solution.py:26
  7.9 109.4 %all-gather.9.cloned.1.call-start = ((), (), s32[]{:S(2)}) async-start(), calls=%async_computation | async-start | bytes 1179648 | tf_op jit(solution)/shard_map/all_gather | solution.py:72
  54.3 7.3 %collective-permute-start.1 = (bf16[128,512]{1,0:T(8,128)(2,1)S(1)}, bf16[128,512]{1,0:T(8,128)(2,1)S(1)}, u32[]{:S(2)}, u32[]{:S(2)}) collective-permute-start(bf16[128,512]{1,0:T(8,128)(2,1)S(1)} %get-tuple-element.135), channel_id=1, source_target_pairs={{0,1},{1,2},{2,3},{3,4},{4,5},{5,6},{6,7},{7,0},{8,9},{9,10},{10,1... | collective-permute-start | bytes 393224 | tf_op jit(solution)/shard_map/while/body/eval_jaxpr/ppermute | solution.py:43
  61.6 6.2 %collective-permute-start.2 = (bf16[128,512]{1,0:T(8,128)(2,1)S(1)}, bf16[128,512]{1,0:T(8,128)(2,1)S(1)}, u32[]{:S(2)}, u32[]{:S(2)}) collective-permute-start(bf16[128,512]{1,0:T(8,128)(2,1)S(1)} %collective-permute-done.1), channel_id=1, source_target_pairs={{0,1},{1,2},{2,3},{3,4},{4,5},{5,6},{6,7},{7,0},{8,9},{9,10},{10,1... | collective-permute-start | bytes 393224 | tf_op jit(solution)/shard_map/while/body/eval_jaxpr/ppermute | solution.py:43
  67.8 6.2 %collective-permute-start.3 = (bf16[128,512]{1,0:T(8,128)(2,1)S(1)}, bf16[128,512]{1,0:T(8,128)(2,1)S(1)}, u32[]{:S(2)}, u32[]{:S(2)}) collective-permute-start(bf16[128,512]{1,0:T(8,128)(2,1)S(1)} %collective-permute-done.2), channel_id=1, source_target_pairs={{0,1},{1,2},{2,3},{3,4},{4,5},{5,6},{6,7},{7,0},{8,9},{9,10},{10,1... | collective-permute-start | bytes 393224 | tf_op jit(solution)/shard_map/while/body/eval_jaxpr/ppermute | solution.py:43
  74.0 6.2 %collective-permute-start.4 = (bf16[128,512]{1,0:T(8,128)(2,1)S(1)}, bf16[128,512]{1,0:T(8,128)(2,1)S(1)}, u32[]{:S(2)}, u32[]{:S(2)}) collective-permute-start(bf16[128,512]{1,0:T(8,128)(2,1)S(1)} %collective-permute-done.3), channel_id=1, source_target_pairs={{0,1},{1,2},{2,3},{3,4},{4,5},{5,6},{6,7},{7,0},{8,9},{9,10},{10,1... | collective-permute-start | bytes 393224 | tf_op jit(solution)/shard_map/while/body/eval_jaxpr/ppermute | solution.py:43
  80.1 6.2 %collective-permute-start.5 = (bf16[128,512]{1,0:T(8,128)(2,1)S(1)}, bf16[128,512]{1,0:T(8,128)(2,1)S(1)}, u32[]{:S(2)}, u32[]{:S(2)}) collective-permute-start(bf16[128,512]{1,0:T(8,128)(2,1)S(1)} %collective-permute-done.4), channel_id=1, source_target_pairs={{0,1},{1,2},{2,3},{3,4},{4,5},{5,6},{6,7},{7,0},{8,9},{9,10},{10,1... | collective-permute-start | bytes 393224 | tf_op jit(solution)/shard_map/while/body/eval_jaxpr/ppermute | solution.py:43
  86.3 6.2 %collective-permute-start.6 = (bf16[128,512]{1,0:T(8,128)(2,1)S(1)}, bf16[128,512]{1,0:T(8,128)(2,1)S(1)}, u32[]{:S(2)}, u32[]{:S(2)}) collective-permute-start(bf16[128,512]{1,0:T(8,128)(2,1)S(1)} %collective-permute-done.5), channel_id=1, source_target_pairs={{0,1},{1,2},{2,3},{3,4},{4,5},{5,6},{6,7},{7,0},{8,9},{9,10},{10,1... | collective-permute-start | bytes 393224 | tf_op jit(solution)/shard_map/while/body/eval_jaxpr/ppermute | solution.py:43
  86.6 6.4 %collective-permute-start = (bf16[1,128,512]{2,1,0:T(8,128)(2,1)S(1)}, bf16[1,128,512]{2,1,0:T(8,128)(2,1)S(1)}, u32[]{:S(2)}, u32[]{:S(2)}) collective-permute-start(bf16[1,128,512]{2,1,0:T(8,128)(2,1)S(1)} %get-tuple-element.144), channel_id=1, source_target_pairs={{0,8},{8,16},{16,24},{1,9},{9,17},{17,25},{2,10},{10,18},{18,26},{... | collective-permute-start | bytes 393224 | tf_op jit(solution)/shard_map/ppermute | solution.py:10
  92.5 6.2 %collective-permute-start.7 = (bf16[128,512]{1,0:T(8,128)(2,1)S(1)}, bf16[128,512]{1,0:T(8,128)(2,1)S(1)}, u32[]{:S(2)}, u32[]{:S(2)}) collective-permute-start(bf16[128,512]{1,0:T(8,128)(2,1)S(1)} %collective-permute-done.6), channel_id=1, source_target_pairs={{0,1},{1,2},{2,3},{3,4},{4,5},{5,6},{6,7},{7,0},{8,9},{9,10},{10,1... | collective-permute-start | bytes 393224 | tf_op jit(solution)/shard_map/while/body/eval_jaxpr/ppermute | solution.py:43
  93.7 104.0 %all-gather.11.cloned.1.call-start = ((), (), s32[]{:S(2)}) async-start(), calls=%async_computation.1 | async-start | bytes 1179648 | tf_op jit(solution)/shard_map/all_gather | solution.py:72
  134.6 6.2 %collective-permute-start.9 = (bf16[128,512]{1,0:T(8,128)(2,1)S(1)}, bf16[128,512]{1,0:T(8,128)(2,1)S(1)}, u32[]{:S(2)}, u32[]{:S(2)}) collective-permute-start(bf16[128,512]{1,0:T(8,128)(2,1)S(1)} %get-tuple-element.124), channel_id=1, source_target_pairs={{0,1},{1,2},{2,3},{3,4},{4,5},{5,6},{6,7},{7,0},{8,9},{9,10},{10,1... | collective-permute-start | bytes 393224 | tf_op jit(solution)/shard_map/while/body/eval_jaxpr/ppermute | solution.py:43
  140.8 6.2 %collective-permute-start.10 = (bf16[128,512]{1,0:T(8,128)(2,1)S(1)}, bf16[128,512]{1,0:T(8,128)(2,1)S(1)}, u32[]{:S(2)}, u32[]{:S(2)}) collective-permute-start(bf16[128,512]{1,0:T(8,128)(2,1)S(1)} %collective-permute-done.9), channel_id=1, source_target_pairs={{0,1},{1,2},{2,3},{3,4},{4,5},{5,6},{6,7},{7,0},{8,9},{9,10},{10,1... | collective-permute-start | bytes 393224 | tf_op jit(solution)/shard_map/while/body/eval_jaxpr/ppermute | solution.py:43
  146.9 6.2 %collective-permute-start.11 = (bf16[128,512]{1,0:T(8,128)(2,1)S(1)}, bf16[128,512]{1,0:T(8,128)(2,1)S(1)}, u32[]{:S(2)}, u32[]{:S(2)}) collective-permute-start(bf16[128,512]{1,0:T(8,128)(2,1)S(1)} %collective-permute-done.10), channel_id=1, source_target_pairs={{0,1},{1,2},{2,3},{3,4},{4,5},{5,6},{6,7},{7,0},{8,9},{9,10},{10,1... | collective-permute-start | bytes 393224 | tf_op jit(solution)/shard_map/while/body/eval_jaxpr/ppermute | solution.py:43
  153.8 6.3 %collective-permute-start.12 = (bf16[128,512]{1,0:T(8,128)(2,1)S(1)}, bf16[128,512]{1,0:T(8,128)(2,1)}, u32[]{:S(2)}, u32[]{:S(2)}) collective-permute-start(bf16[128,512]{1,0:T(8,128)(2,1)S(1)} %collective-permute-done.11), channel_id=1, source_target_pairs={{0,1},{1,2},{2,3},{3,4},{4,5},{5,6},{6,7},{7,0},{8,9},{9,10},{10,1... | collective-permute-start | bytes 393224 | tf_op jit(solution)/shard_map/while/body/eval_jaxpr/ppermute | solution.py:43
  160.1 6.5 %collective-permute-start.13 = (bf16[128,512]{1,0:T(8,128)(2,1)}, bf16[128,512]{1,0:T(8,128)(2,1)}, u32[]{:S(2)}, u32[]{:S(2)}) collective-permute-start(bf16[128,512]{1,0:T(8,128)(2,1)} %collective-permute-done.12), channel_id=1, source_target_pairs={{0,1},{1,2},{2,3},{3,4},{4,5},{5,6},{6,7},{7,0},{8,9},{9,10},{10,1... | collective-permute-start | bytes 393224 | tf_op jit(solution)/shard_map/while/body/eval_jaxpr/ppermute | solution.py:43
  166.6 6.5 %collective-permute-start.14 = (bf16[128,512]{1,0:T(8,128)(2,1)}, bf16[128,512]{1,0:T(8,128)(2,1)}, u32[]{:S(2)}, u32[]{:S(2)}) collective-permute-start(bf16[128,512]{1,0:T(8,128)(2,1)} %collective-permute-done.13), channel_id=1, source_target_pairs={{0,1},{1,2},{2,3},{3,4},{4,5},{5,6},{6,7},{7,0},{8,9},{9,10},{10,1... | collective-permute-start | bytes 393224 | tf_op jit(solution)/shard_map/while/body/eval_jaxpr/ppermute | solution.py:43
  166.9 6.2 %collective-permute-start.8 = (bf16[1,128,512]{2,1,0:T(8,128)(2,1)S(1)}, bf16[1,128,512]{2,1,0:T(8,128)(2,1)S(1)}, u32[]{:S(2)}, u32[]{:S(2)}) collective-permute-start(bf16[1,128,512]{2,1,0:T(8,128)(2,1)S(1)} %get-tuple-element.134), channel_id=1, source_target_pairs={{0,8},{8,16},{16,24},{1,9},{9,17},{17,25},{2,10},{10,18},{18,26},{... | collective-permute-start | bytes 393224 | tf_op jit(solution)/shard_map/ppermute | solution.py:10
  173.1 6.4 %collective-permute-start.15 = (bf16[128,512]{1,0:T(8,128)(2,1)}, bf16[128,512]{1,0:T(8,128)(2,1)S(1)}, u32[]{:S(2)}, u32[]{:S(2)}) collective-permute-start(bf16[128,512]{1,0:T(8,128)(2,1)} %collective-permute-done.14), channel_id=1, source_target_pairs={{0,1},{1,2},{2,3},{3,4},{4,5},{5,6},{6,7},{7,0},{8,9},{9,10},{10,1... | collective-permute-start | bytes 393224 | tf_op jit(solution)/shard_map/while/body/eval_jaxpr/ppermute | solution.py:43
  173.8 104.7 %all-gather.13.cloned.1.call-start = ((), (), s32[]{:S(2)}) async-start(), calls=%async_computation.2 | async-start | bytes 1179648 | tf_op jit(solution)/shard_map/all_gather | solution.py:72
  215.0 6.2 %collective-permute-start.17 = (bf16[128,512]{1,0:T(8,128)(2,1)S(1)}, bf16[128,512]{1,0:T(8,128)(2,1)S(1)}, u32[]{:S(2)}, u32[]{:S(2)}) collective-permute-start(bf16[128,512]{1,0:T(8,128)(2,1)S(1)} %get-tuple-element.113), channel_id=1, source_target_pairs={{0,1},{1,2},{2,3},{3,4},{4,5},{5,6},{6,7},{7,0},{8,9},{9,10},{10,1... | collective-permute-start | bytes 393224 | tf_op jit(solution)/shard_map/while/body/eval_jaxpr/ppermute | solution.py:43
  221.3 6.2 %collective-permute-start.18 = (bf16[128,512]{1,0:T(8,128)(2,1)S(1)}, bf16[128,512]{1,0:T(8,128)(2,1)S(1)}, u32[]{:S(2)}, u32[]{:S(2)}) collective-permute-start(bf16[128,512]{1,0:T(8,128)(2,1)S(1)} %collective-permute-done.17), channel_id=1, source_target_pairs={{0,1},{1,2},{2,3},{3,4},{4,5},{5,6},{6,7},{7,0},{8,9},{9,10},{10,1... | collective-permute-start | bytes 393224 | tf_op jit(solution)/shard_map/while/body/eval_jaxpr/ppermute | solution.py:43
  227.5 6.2 %collective-permute-start.19 = (bf16[128,512]{1,0:T(8,128)(2,1)S(1)}, bf16[128,512]{1,0:T(8,128)(2,1)S(1)}, u32[]{:S(2)}, u32[]{:S(2)}) collective-permute-start(bf16[128,512]{1,0:T(8,128)(2,1)S(1)} %collective-permute-done.18), channel_id=1, source_target_pairs={{0,1},{1,2},{2,3},{3,4},{4,5},{5,6},{6,7},{7,0},{8,9},{9,10},{10,1... | collective-permute-start | bytes 393224 | tf_op jit(solution)/shard_map/while/body/eval_jaxpr/ppermute | solution.py:43
  233.7 6.2 %collective-permute-start.20 = (bf16[128,512]{1,0:T(8,128)(2,1)S(1)}, bf16[128,512]{1,0:T(8,128)(2,1)S(1)}, u32[]{:S(2)}, u32[]{:S(2)}) collective-permute-start(bf16[128,512]{1,0:T(8,128)(2,1)S(1)} %collective-permute-done.19), channel_id=1, source_target_pairs={{0,1},{1,2},{2,3},{3,4},{4,5},{5,6},{6,7},{7,0},{8,9},{9,10},{10,1... | collective-permute-start | bytes 393224 | tf_op jit(solution)/shard_map/while/body/eval_jaxpr/ppermute | solution.py:43
  239.8 6.3 %collective-permute-start.21 = (bf16[128,512]{1,0:T(8,128)(2,1)S(1)}, bf16[128,512]{1,0:T(8,128)(2,1)}, u32[]{:S(2)}, u32[]{:S(2)}) collective-permute-start(bf16[128,512]{1,0:T(8,128)(2,1)S(1)} %collective-permute-done.20), channel_id=1, source_target_pairs={{0,1},{1,2},{2,3},{3,4},{4,5},{5,6},{6,7},{7,0},{8,9},{9,10},{10,1... | collective-permute-start | bytes 393224 | tf_op jit(solution)/shard_map/while/body/eval_jaxpr/ppermute | solution.py:43
  246.1 6.5 %collective-permute-start.22 = (bf16[128,512]{1,0:T(8,128)(2,1)}, bf16[128,512]{1,0:T(8,128)(2,1)}, u32[]{:S(2)}, u32[]{:S(2)}) collective-permute-start(bf16[128,512]{1,0:T(8,128)(2,1)} %collective-permute-done.21), channel_id=1, source_target_pairs={{0,1},{1,2},{2,3},{3,4},{4,5},{5,6},{6,7},{7,0},{8,9},{9,10},{10,1... | collective-permute-start | bytes 393224 | tf_op jit(solution)/shard_map/while/body/eval_jaxpr/ppermute | solution.py:43
  252.7 6.4 %collective-permute-start.23 = (bf16[128,512]{1,0:T(8,128)(2,1)}, bf16[128,512]{1,0:T(8,128)(2,1)S(1)}, u32[]{:S(2)}, u32[]{:S(2)}) collective-permute-start(bf16[128,512]{1,0:T(8,128)(2,1)} %collective-permute-done.22), channel_id=1, source_target_pairs={{0,1},{1,2},{2,3},{3,4},{4,5},{5,6},{6,7},{7,0},{8,9},{9,10},{10,1... | collective-permute-start | bytes 393224 | tf_op jit(solution)/shard_map/while/body/eval_jaxpr/ppermute | solution.py:43
  255.1 103.8 %all-gather.15.cloned.1.call-start = ((), (), s32[]{:S(2)}) async-start(), calls=%async_computation.3 | async-start | bytes 1179648 | tf_op jit(solution)/shard_map/all_gather | solution.py:72
  295.8 6.2 %collective-permute-start.25 = (bf16[128,512]{1,0:T(8,128)(2,1)S(1)}, bf16[128,512]{1,0:T(8,128)(2,1)S(1)}, u32[]{:S(2)}, u32[]{:S(2)}) collective-permute-start(bf16[128,512]{1,0:T(8,128)(2,1)S(1)} %get-tuple-element.108), channel_id=1, source_target_pairs={{0,1},{1,2},{2,3},{3,4},{4,5},{5,6},{6,7},{7,0},{8,9},{9,10},{10,1... | collective-permute-start | bytes 393224 | tf_op jit(solution)/shard_map/while/body/eval_jaxpr/ppermute | solution.py:43
  302.0 6.2 %collective-permute-start.26 = (bf16[128,512]{1,0:T(8,128)(2,1)S(1)}, bf16[128,512]{1,0:T(8,128)(2,1)S(1)}, u32[]{:S(2)}, u32[]{:S(2)}) collective-permute-start(bf16[128,512]{1,0:T(8,128)(2,1)S(1)} %collective-permute-done.25), channel_id=1, source_target_pairs={{0,1},{1,2},{2,3},{3,4},{4,5},{5,6},{6,7},{7,0},{8,9},{9,10},{10,1... | collective-permute-start | bytes 393224 | tf_op jit(solution)/shard_map/while/body/eval_jaxpr/ppermute | solution.py:43
  308.2 6.2 %collective-permute-start.27 = (bf16[128,512]{1,0:T(8,128)(2,1)S(1)}, bf16[128,512]{1,0:T(8,128)(2,1)S(1)}, u32[]{:S(2)}, u32[]{:S(2)}) collective-permute-start(bf16[128,512]{1,0:T(8,128)(2,1)S(1)} %collective-permute-done.26), channel_id=1, source_target_pairs={{0,1},{1,2},{2,3},{3,4},{4,5},{5,6},{6,7},{7,0},{8,9},{9,10},{10,1... | collective-permute-start | bytes 393224 | tf_op jit(solution)/shard_map/while/body/eval_jaxpr/ppermute | solution.py:43
  326.8 6.3 %collective-permute-start.30 = (bf16[128,512]{1,0:T(8,128)(2,1)S(1)}, bf16[128,512]{1,0:T(8,128)(2,1)}, u32[]{:S(2)}, u32[]{:S(2)}) collective-permute-start(bf16[128,512]{1,0:T(8,128)(2,1)S(1)} %collective-permute-done.29), channel_id=1, source_target_pairs={{0,1},{1,2},{2,3},{3,4},{4,5},{5,6},{6,7},{7,0},{8,9},{9,10},{10,1... | collective-permute-start | bytes 393224 | tf_op jit(solution)/shard_map/while/body/eval_jaxpr/ppermute | solution.py:43
  333.1 6.4 %collective-permute-start.31 = (bf16[128,512]{1,0:T(8,128)(2,1)}, bf16[128,512]{1,0:T(8,128)(2,1)S(1)}, u32[]{:S(2)}, u32[]{:S(2)}) collective-permute-start(bf16[128,512]{1,0:T(8,128)(2,1)} %collective-permute-done.30), channel_id=1, source_target_pairs={{0,1},{1,2},{2,3},{3,4},{4,5},{5,6},{6,7},{7,0},{8,9},{9,10},{10,1... | collective-permute-start | bytes 393224 | tf_op jit(solution)/shard_map/while/body/eval_jaxpr/ppermute | solution.py:43
  335.5 107.4 %all-gather.17.cloned.1.call-start = ((), (), s32[]{:S(2)}) async-start(), calls=%async_computation.4 | async-start | bytes 1179648 | tf_op jit(solution)/shard_map/all_gather | solution.py:72
  377.1 6.2 %collective-permute-start.33 = (bf16[128,512]{1,0:T(8,128)(2,1)S(1)}, bf16[128,512]{1,0:T(8,128)(2,1)S(1)}, u32[]{:S(2)}, u32[]{:S(2)}) collective-permute-start(bf16[128,512]{1,0:T(8,128)(2,1)S(1)} %get-tuple-element.97), channel_id=1, source_target_pairs={{0,1},{1,2},{2,3},{3,4},{4,5},{5,6},{6,7},{7,0},{8,9},{9,10},{10,1... | collective-permute-start | bytes 393224 | tf_op jit(solution)/shard_map/while/body/eval_jaxpr/ppermute | solution.py:43
  384.0 6.2 %collective-permute-start.34 = (bf16[128,512]{1,0:T(8,128)(2,1)S(1)}, bf16[128,512]{1,0:T(8,128)(2,1)S(1)}, u32[]{:S(2)}, u32[]{:S(2)}) collective-permute-start(bf16[128,512]{1,0:T(8,128)(2,1)S(1)} %collective-permute-done.33), channel_id=1, source_target_pairs={{0,1},{1,2},{2,3},{3,4},{4,5},{5,6},{6,7},{7,0},{8,9},{9,10},{10,1... | collective-permute-start | bytes 393224 | tf_op jit(solution)/shard_map/while/body/eval_jaxpr/ppermute | solution.py:43
  390.8 6.2 %collective-permute-start.35 = (bf16[128,512]{1,0:T(8,128)(2,1)S(1)}, bf16[128,512]{1,0:T(8,128)(2,1)S(1)}, u32[]{:S(2)}, u32[]{:S(2)}) collective-permute-start(bf16[128,512]{1,0:T(8,128)(2,1)S(1)} %collective-permute-done.34), channel_id=1, source_target_pairs={{0,1},{1,2},{2,3},{3,4},{4,5},{5,6},{6,7},{7,0},{8,9},{9,10},{10,1... | collective-permute-start | bytes 393224 | tf_op jit(solution)/shard_map/while/body/eval_jaxpr/ppermute | solution.py:43
  397.7 6.3 %collective-permute-start.36 = (bf16[128,512]{1,0:T(8,128)(2,1)S(1)}, bf16[128,512]{1,0:T(8,128)(2,1)}, u32[]{:S(2)}, u32[]{:S(2)}) collective-permute-start(bf16[128,512]{1,0:T(8,128)(2,1)S(1)} %collective-permute-done.35), channel_id=1, source_target_pairs={{0,1},{1,2},{2,3},{3,4},{4,5},{5,6},{6,7},{7,0},{8,9},{9,10},{10,1... | collective-permute-start | bytes 393224 | tf_op jit(solution)/shard_map/while/body/eval_jaxpr/ppermute | solution.py:43
  404.0 6.5 %collective-permute-start.37 = (bf16[128,512]{1,0:T(8,128)(2,1)}, bf16[128,512]{1,0:T(8,128)(2,1)}, u32[]{:S(2)}, u32[]{:S(2)}) collective-permute-start(bf16[128,512]{1,0:T(8,128)(2,1)} %collective-permute-done.36), channel_id=1, source_target_pairs={{0,1},{1,2},{2,3},{3,4},{4,5},{5,6},{6,7},{7,0},{8,9},{9,10},{10,1... | collective-permute-start | bytes 393224 | tf_op jit(solution)/shard_map/while/body/eval_jaxpr/ppermute | solution.py:43
  410.5 6.5 %collective-permute-start.38 = (bf16[128,512]{1,0:T(8,128)(2,1)}, bf16[128,512]{1,0:T(8,128)(2,1)}, u32[]{:S(2)}, u32[]{:S(2)}) collective-permute-start(bf16[128,512]{1,0:T(8,128)(2,1)} %collective-permute-done.37), channel_id=1, source_target_pairs={{0,1},{1,2},{2,3},{3,4},{4,5},{5,6},{6,7},{7,0},{8,9},{9,10},{10,1... | collective-permute-start | bytes 393224 | tf_op jit(solution)/shard_map/while/body/eval_jaxpr/ppermute | solution.py:43
  412.5 6.5 %collective-permute-start.32 = (bf16[1,128,512]{2,1,0:T(8,128)(2,1)}, bf16[1,128,512]{2,1,0:T(8,128)(2,1)S(1)}, u32[]{:S(2)}, u32[]{:S(2)}) collective-permute-start(bf16[1,128,512]{2,1,0:T(8,128)(2,1)} %get-tuple-element.100), channel_id=1, source_target_pairs={{0,8},{8,16},{16,24},{1,9},{9,17},{17,25},{2,10},{10,18},{18,26},{... | collective-permute-start | bytes 393224 | tf_op jit(solution)/shard_map/ppermute | solution.py:10
  417.0 6.4 %collective-permute-start.39 = (bf16[128,512]{1,0:T(8,128)(2,1)}, bf16[128,512]{1,0:T(8,128)(2,1)S(1)}, u32[]{:S(2)}, u32[]{:S(2)}) collective-permute-start(bf16[128,512]{1,0:T(8,128)(2,1)} %collective-permute-done.38), channel_id=1, source_target_pairs={{0,1},{1,2},{2,3},{3,4},{4,5},{5,6},{6,7},{7,0},{8,9},{9,10},{10,1... | collective-permute-start | bytes 393224 | tf_op jit(solution)/shard_map/while/body/eval_jaxpr/ppermute | solution.py:43
  419.7 103.7 %all-gather.19.cloned.1.call-start = ((), (), s32[]{:S(2)}) async-start(), calls=%async_computation.5 | async-start | bytes 1179648 | tf_op jit(solution)/shard_map/all_gather | solution.py:72
  460.8 6.2 %collective-permute-start.41 = (bf16[128,512]{1,0:T(8,128)(2,1)S(1)}, bf16[128,512]{1,0:T(8,128)(2,1)S(1)}, u32[]{:S(2)}, u32[]{:S(2)}) collective-permute-start(bf16[128,512]{1,0:T(8,128)(2,1)S(1)} %fusion.129), channel_id=1, source_target_pairs={{0,1},{1,2},{2,3},{3,4},{4,5},{5,6},{6,7},{7,0},{8,9},{9,10},{10,1... | collective-permute-start | bytes 393224 | tf_op jit(solution)/shard_map/while/body/eval_jaxpr/ppermute | solution.py:43
  485.6 6.3 %collective-permute-start.45 = (bf16[128,512]{1,0:T(8,128)(2,1)S(1)}, bf16[128,512]{1,0:T(8,128)(2,1)}, u32[]{:S(2)}, u32[]{:S(2)}) collective-permute-start(bf16[128,512]{1,0:T(8,128)(2,1)S(1)} %collective-permute-done.44), channel_id=1, source_target_pairs={{0,1},{1,2},{2,3},{3,4},{4,5},{5,6},{6,7},{7,0},{8,9},{9,10},{10,1... | collective-permute-start | bytes 393224 | tf_op jit(solution)/shard_map/while/body/eval_jaxpr/ppermute | solution.py:43
  491.9 6.5 %collective-permute-start.46 = (bf16[128,512]{1,0:T(8,128)(2,1)}, bf16[128,512]{1,0:T(8,128)(2,1)}, u32[]{:S(2)}, u32[]{:S(2)}) collective-permute-start(bf16[128,512]{1,0:T(8,128)(2,1)} %collective-permute-done.45), channel_id=1, source_target_pairs={{0,1},{1,2},{2,3},{3,4},{4,5},{5,6},{6,7},{7,0},{8,9},{9,10},{10,1... | collective-permute-start | bytes 393224 | tf_op jit(solution)/shard_map/while/body/eval_jaxpr/ppermute | solution.py:43
  493.3 6.2 %collective-permute-start.40 = (bf16[1,128,512]{2,1,0:T(8,128)(2,1)S(1)}, bf16[1,128,512]{2,1,0:T(8,128)(2,1)}, u32[]{:S(2)}, u32[]{:S(2)}) collective-permute-start(bf16[1,128,512]{2,1,0:T(8,128)(2,1)S(1)} %get-tuple-element.96), channel_id=1, source_target_pairs={{0,8},{8,16},{16,24},{1,9},{9,17},{17,25},{2,10},{10,18},{18,26},{... | collective-permute-start | bytes 393224 | tf_op jit(solution)/shard_map/ppermute | solution.py:10
  498.4 6.8 %collective-permute-start.47 = (bf16[128,512]{1,0:T(8,128)(2,1)}, bf16[128,512]{1,0:T(8,128)(2,1)}, u32[]{:S(2)}, u32[]{:S(2)}) collective-permute-start(bf16[128,512]{1,0:T(8,128)(2,1)} %collective-permute-done.46), channel_id=1, source_target_pairs={{0,1},{1,2},{2,3},{3,4},{4,5},{5,6},{6,7},{7,0},{8,9},{9,10},{10,1... | collective-permute-start | bytes 393224 | tf_op jit(solution)/shard_map/while/body/eval_jaxpr/ppermute | solution.py:43
  (39 other events, 863.9 us)
Sparse Core Ops, SparseCore 0:
  9.6 24.9 all-gather.20
  93.8 23.4 all-gather.8
  173.9 23.7 all-gather.10
  255.2 23.2 all-gather.12
  335.6 23.2 all-gather.14
  419.8 23.0 all-gather.16
  499.7 23.6 all-gather.18
